TPU v7x, 512 devices: a whole 4x4x16 slice. The times are simulated.
512 devices in a mesh: pipe: 8 (over y, core), ctx: 16 (over z), head: 4 (over x).
Axes of the slice: x: 4, y: 4, z: 16, core: 2. Of those that a mesh axis runs over, the one named last changes fastest.
Arguments:
- x_in: bfloat16 [8, 12288, 4096], P('pipe', 'ctx', 'head'), may hold values from -6 to 6
- b_in: bfloat16 [8, 12288, 512], P('pipe', 'ctx', 'head'), may hold values from -6 to 6
- c_in: bfloat16 [8, 12288, 512], P('pipe', 'ctx', 'head'), may hold values from -6 to 6
- z_in: bfloat16 [8, 12288, 4096], P('pipe', 'ctx', 'head'), may hold values from -6 to 6
- dt_raw: float32 [8, 12288, 64], P('pipe', 'ctx', 'head'), may hold values from -5 to 5
- seg_ids: int32 [8, 12288], P('pipe', 'ctx'), may hold values from 0 to 3, never falling along the last dimension, each value on 1 to 6144 neighbouring positions
- conv_x: float32 [8, 4, 4096], P('pipe', None, 'head'), may hold values from -3 to 3
- conv_bc: float32 [8, 2, 4, 512], P('pipe', None, None, 'head'), may hold values from -3 to 3
- decay_rate: float32 [8, 64], P('pipe', 'head'), may hold values from 8.138021e-06 to 0.041666667, as said below
- dt_bias: float32 [8, 64], P('pipe', 'head'), may hold values from -1 to 1
- skip_d: float32 [8, 64], P('pipe', 'head'), may hold values from 0.5 to 2
- norm_gain: float32 [8, 4096], P('pipe', 'head'), may hold values from 0.5 to 1.5
Outputs:
- next_rows: bfloat16 [8, 12288, 4096], P('pipe', ('ctx', 'head'))
Inputs may be any that keep to these rules, and one draw needn't show every extreme that they name: `seg_ids`: along each section's tokens ids never fall; every request holds 1 to 6144 tokens and one holds exactly 6144. `decay_rate`: positive rates.
All inputs are finite; a program needn't handle non-finite values.
Results may differ from a plain program's by a relative error of at most 0.005.
Values may be sent and summed in bfloat16 or wider, within the bound.
A program may use at most 128 MiB of HBM per device.

v0:
```python
import jax
import jax.numpy as jnp
from jax import lax
from jax.sharding import PartitionSpec as P

HEADS = 64
GROUPS = 4


def passed_along(value, axis, steps):
    count = lax.axis_size(axis)
    first, last = (max(0, -steps), min(count, count - steps))
    return lax.ppermute(value, axis, [(source, source + steps) for source in range(first, last)])


def carried_in(part, axis, combine, identity):
    place = lax.axis_index(axis)
    gathered = jax.tree.map(lambda a: lax.all_gather(a, axis), part)
    state = jax.tree.map(lambda a, e: jnp.zeros_like(a) + jnp.asarray(e, a.dtype), part, identity)

    def one(lap, state):
        return combine(
            state, jax.tree.map(lambda a: lax.dynamic_index_in_dim(a, lap, 0, False), gathered)
        )

    return lax.fori_loop(0, place, one, state)


def shifted(value, axis, steps):
    count = lax.axis_size(axis)
    pairs = [(source, (source + steps) % count) for source in range(count)]
    return lax.ppermute(value, axis, pairs)


def conv_silu(current, previous, kernel, segments, prev_segments):
    length = current.shape[0]
    extended = jnp.concatenate([previous, current], axis=0)
    ext_segments = jnp.concatenate([prev_segments, segments], axis=0)
    total = jnp.zeros(current.shape, jnp.float32)
    for offset in range(kernel.shape[0]):
        same = (ext_segments[offset : offset + length] == segments)[:, None]
        total = total + jnp.where(same, kernel[offset] * extended[offset : offset + length], 0.0)
    return jax.nn.silu(total).astype(jnp.bfloat16)


def shards(
    x_in, b_in, c_in, z_in, dt_raw, seg_ids, conv_x, conv_bc, decay_rate, dt_bias, skip_d, norm_gain
):
    values = x_in[0]
    key_rows = b_in[0]
    query_rows = c_in[0]
    segments = seg_ids[0]
    length = values.shape[0]
    margin = conv_x.shape[1] - 1
    prev_values, prev_keys, prev_queries, prev_segments = passed_along(
        (
            values[length - margin :],
            key_rows[length - margin :],
            query_rows[length - margin :],
            segments[length - margin :],
        ),
        "ctx",
        1,
    )
    mixed_x = conv_silu(values, prev_values, conv_x[0], segments, prev_segments)
    mixed_b = conv_silu(key_rows, prev_keys, conv_bc[0, 0], segments, prev_segments)
    mixed_c = conv_silu(query_rows, prev_queries, conv_bc[0, 1], segments, prev_segments)
    heads_local = decay_rate.shape[1]
    per_group = HEADS // GROUPS
    groups_local = heads_local // per_group
    head_width = values.shape[1] // heads_local
    state_width = key_rows.shape[1] // groups_local
    steps_dt = jax.nn.softplus(dt_raw[0] + dt_bias[0][None, :])
    cum = jnp.cumsum(-steps_dt * decay_rate[0][None, :], axis=0)
    prior = prev_segments[margin - 1]
    last = segments[length - 1]
    head_x = mixed_x.reshape(length, heads_local, head_width)
    group_b = mixed_b.reshape(length, groups_local, state_width)
    group_c = mixed_c.reshape(length, groups_local, state_width)
    scores = jnp.einsum("tgn,sgn->gts", group_c, group_b, preferred_element_type=jnp.float32)
    position = jnp.arange(length)
    causal = (position[:, None] >= position[None, :]) & (segments[:, None] == segments[None, :])

    def one_head(index):
        score = lax.dynamic_index_in_dim(scores, index // per_group, 0, keepdims=False)
        cum_head = lax.dynamic_index_in_dim(cum, index, 1, keepdims=False)
        step_head = lax.dynamic_index_in_dim(steps_dt, index, 1, keepdims=False)
        x_head = lax.dynamic_index_in_dim(head_x, index, 1, keepdims=False)
        gap = jnp.where(causal, cum_head[:, None] - cum_head[None, :], 0.0)
        weights = jnp.where(causal, score * jnp.exp(gap) * step_head[None, :], 0.0).astype(
            jnp.bfloat16
        )
        return jnp.dot(weights, x_head, preferred_element_type=jnp.float32)

    intra = lax.map(one_head, jnp.arange(heads_local))
    tail = (
        jnp.exp(cum[length - 1][None, :] - cum)
        * steps_dt
        * (segments == last).astype(jnp.float32)[:, None]
    )
    scaled = (head_x * tail[:, :, None]).astype(jnp.bfloat16)
    local = jnp.einsum(
        "sgkp,sgn->gkpn",
        scaled.reshape(length, groups_local, per_group, head_width),
        group_b,
        preferred_element_type=jnp.float32,
    ).reshape(heads_local, head_width, state_width)
    through = jnp.exp(cum[length - 1]) * (last == prior).astype(jnp.float32)

    def link(earlier, later):
        return (earlier[0] * later[0], later[0][:, None, None] * earlier[1] + later[1])

    carried = carried_in(
        (through, local), "ctx", link, (jnp.ones_like(through), jnp.zeros_like(local))
    )[1]
    inter = jnp.einsum(
        "tgn,gkpn->tgkp",
        group_c.astype(jnp.float32),
        carried.reshape(groups_local, per_group, head_width, state_width),
        precision=lax.Precision.HIGHEST,
    ).reshape(length, heads_local, head_width)
    entry = jnp.exp(cum) * (segments == prior).astype(jnp.float32)[:, None]
    mixed = (
        jnp.transpose(intra, (1, 0, 2))
        + entry[:, :, None] * inter
        + skip_d[0][None, :, None] * head_x
    )
    gated = mixed.reshape(length, heads_local * head_width) * jax.nn.silu(
        z_in[0].astype(jnp.float32)
    )
    grouped = gated.reshape(length, groups_local, per_group * head_width)
    stats = jnp.mean(grouped * grouped, axis=-1, keepdims=True)
    normed = (grouped * lax.rsqrt(stats + 1e-05)).reshape(length, heads_local * head_width)
    section_out = (normed * norm_gain[0][None, :]).astype(jnp.bfloat16)
    regrouped = lax.all_to_all(section_out, "head", split_axis=0, concat_axis=1, tiled=True)
    moved = shifted(regrouped, "pipe", 1)
    return moved[None]


def solution(mesh):
    placed = (
        P("pipe", "ctx", "head"),
        P("pipe", "ctx", "head"),
        P("pipe", "ctx", "head"),
        P("pipe", "ctx", "head"),
        P("pipe", "ctx", "head"),
        P("pipe", "ctx"),
        P("pipe", None, "head"),
        P("pipe", None, None, "head"),
        P("pipe", "head"),
        P("pipe", "head"),
        P("pipe", "head"),
        P("pipe", "head"),
    )
    return jax.shard_map(
        shards,
        mesh=mesh,
        in_specs=placed,
        out_specs=P("pipe", ("ctx", "head"), None),
        check_vma=False,
    )
```

profile of v0, /device:TPU:480, one launch (start us, length us, event | category | flops | bytes accessed | tf_op | source)
XLA Modules:
  0.0 252.6 jit_solution(8397537602593841685)
XLA Ops:
  24.2 4.5 %fusion.20 = (bf16[768,1024]{0,1:T(8,128)(2,1)S(1)}, bf16[768,1024]{0,1:T(8,128)(2,1)S(1)}) fusion(f32[768,16]{0,1:T(8,128)S(1)} %get-tuple-element.155, bf16[768,1024]{0,1:T(8,128)(2,1)S(1)} %bitcast.144, f32[1024]{0:T(1024)} %bitcast.157, bf16[3,1024]{0,1:T(8,128)(2,1)S(1)} %collective-permute-done.3, f32[1024]{0:T(1024)} %bitcast.158, ...), kind=kLoop, calls=%fused_computation.22 | loop fusion | flops 24379392 | bytes 4792576 | tf_op jit(solution)/shard_map/convert_element_type | solution.py:101
  38.1 31.1 %all-gather.1 = f32[16,1,16]{2,1,0:T(1,128)S(1)} all-gather(f32[1,1,16]{2,1,0:T(1,128)S(1)} %bitcast.161), channel_id=1, replica_groups=mesh['pipe'=8,'ctx'=16,'head'=4] {'ctx'}, dimensions={0}, use_global_device_ids=true | all-gather | bytes 1088 | tf_op jit(solution)/shard_map/all_gather | solution.py:18
  69.8 3.9 %convolution_bitcast_fusion = f32[1,768,768]{2,1,0:T(8,128)} fusion(bf16[768,128]{1,0:T(8,128)(2,1)} %bitcast.166, bf16[3,128]{1,0:T(4,128)(2,1)} %copy-done.31, f32[128]{0:T(128)S(1)} %copy-done.17, f32[128]{0:T(128)S(1)} %copy-done.18, f32[128]{0:T(128)S(1)} %copy-done.19, f32[128]{0:T(128)S(1)} %copy-done.20, pred[768]{0:T(1024)(128)(4,1)S(1)} %copy-done.9, ...), kind=kOutput, calls=%fused_computation.30 | convolution fusion | flops 156499968 | bytes 2764288 | tf_op jit(solution)/shard_map/tgn,sgn->gts/dot_general | solution.py:80
  73.7 93.5 %while.24 = (s32[]{:T(128)}, f32[16,768,64]{1,2,0:T(8,128)}, f32[1,768,768]{2,1,0:T(8,128)}, s32[16]{0:T(128)S(1)}, f32[768,16]{0,1:T(8,128)S(1)}, /*index=5*/f3...) while((s32[]{:T(128)}, f32[16,768,64]{1,2,0:T(8,128)}, ...), condition=%wide.region_3.4_spmd.clone, body=%wide.region_2.3_spmd.clone.sunk | while | flops 80805888 | bytes 2687651 | solution.py:95
  76.5 3.1 %fusion.38 = f32[16,768,64]{1,2,0:T(8,128)} fusion(f32[16,768,64]{1,2,0:T(8,128)} %get-tuple-element.299, s32[]{:T(128)} %get-tuple-element.298, f32[1,768,768]{2,1,0:T(8,128)} %get-tuple-element.311, s32[768]{0:T(1024)S(1)} %get-tuple-element.316, f32[768]{0:T(1024)S(1)} %get-tuple-element.261, f32[768]{0:T(1024)S(1)} %get-tuple-element.262, ...), kind=kOutput, calls=%fused_computation.11.clone.1 | convolution fusion | flops 80805888 | bytes 2675204 | tf_op jit(solution)/shard_map/while/body/eval_jaxpr/dot_general | solution.py:93
  82.3 3.1 %fusion.38 = f32[16,768,64]{1,2,0:T(8,128)} fusion(f32[16,768,64]{1,2,0:T(8,128)} %get-tuple-element.299, s32[]{:T(128)} %get-tuple-element.298, f32[1,768,768]{2,1,0:T(8,128)} %get-tuple-element.311, s32[768]{0:T(1024)S(1)} %get-tuple-element.316, f32[768]{0:T(1024)S(1)} %get-tuple-element.261, f32[768]{0:T(1024)S(1)} %get-tuple-element.262, ...), kind=kOutput, calls=%fused_computation.11.clone.1 | convolution fusion | flops 80805888 | bytes 2675204 | tf_op jit(solution)/shard_map/while/body/eval_jaxpr/dot_general | solution.py:93
  88.2 3.1 %fusion.38 = f32[16,768,64]{1,2,0:T(8,128)} fusion(f32[16,768,64]{1,2,0:T(8,128)} %get-tuple-element.299, s32[]{:T(128)} %get-tuple-element.298, f32[1,768,768]{2,1,0:T(8,128)} %get-tuple-element.311, s32[768]{0:T(1024)S(1)} %get-tuple-element.316, f32[768]{0:T(1024)S(1)} %get-tuple-element.261, f32[768]{0:T(1024)S(1)} %get-tuple-element.262, ...), kind=kOutput, calls=%fused_computation.11.clone.1 | convolution fusion | flops 80805888 | bytes 2675204 | tf_op jit(solution)/shard_map/while/body/eval_jaxpr/dot_general | solution.py:93
  94.0 3.1 %fusion.38 = f32[16,768,64]{1,2,0:T(8,128)} fusion(f32[16,768,64]{1,2,0:T(8,128)} %get-tuple-element.299, s32[]{:T(128)} %get-tuple-element.298, f32[1,768,768]{2,1,0:T(8,128)} %get-tuple-element.311, s32[768]{0:T(1024)S(1)} %get-tuple-element.316, f32[768]{0:T(1024)S(1)} %get-tuple-element.261, f32[768]{0:T(1024)S(1)} %get-tuple-element.262, ...), kind=kOutput, calls=%fused_computation.11.clone.1 | convolution fusion | flops 80805888 | bytes 2675204 | tf_op jit(solution)/shard_map/while/body/eval_jaxpr/dot_general | solution.py:93
  99.9 3.1 %fusion.38 = f32[16,768,64]{1,2,0:T(8,128)} fusion(f32[16,768,64]{1,2,0:T(8,128)} %get-tuple-element.299, s32[]{:T(128)} %get-tuple-element.298, f32[1,768,768]{2,1,0:T(8,128)} %get-tuple-element.311, s32[768]{0:T(1024)S(1)} %get-tuple-element.316, f32[768]{0:T(1024)S(1)} %get-tuple-element.261, f32[768]{0:T(1024)S(1)} %get-tuple-element.262, ...), kind=kOutput, calls=%fused_computation.11.clone.1 | convolution fusion | flops 80805888 | bytes 2675204 | tf_op jit(solution)/shard_map/while/body/eval_jaxpr/dot_general | solution.py:93
  105.7 3.1 %fusion.38 = f32[16,768,64]{1,2,0:T(8,128)} fusion(f32[16,768,64]{1,2,0:T(8,128)} %get-tuple-element.299, s32[]{:T(128)} %get-tuple-element.298, f32[1,768,768]{2,1,0:T(8,128)} %get-tuple-element.311, s32[768]{0:T(1024)S(1)} %get-tuple-element.316, f32[768]{0:T(1024)S(1)} %get-tuple-element.261, f32[768]{0:T(1024)S(1)} %get-tuple-element.262, ...), kind=kOutput, calls=%fused_computation.11.clone.1 | convolution fusion | flops 80805888 | bytes 2675204 | tf_op jit(solution)/shard_map/while/body/eval_jaxpr/dot_general | solution.py:93
  111.6 3.1 %fusion.38 = f32[16,768,64]{1,2,0:T(8,128)} fusion(f32[16,768,64]{1,2,0:T(8,128)} %get-tuple-element.299, s32[]{:T(128)} %get-tuple-element.298, f32[1,768,768]{2,1,0:T(8,128)} %get-tuple-element.311, s32[768]{0:T(1024)S(1)} %get-tuple-element.316, f32[768]{0:T(1024)S(1)} %get-tuple-element.261, f32[768]{0:T(1024)S(1)} %get-tuple-element.262, ...), kind=kOutput, calls=%fused_computation.11.clone.1 | convolution fusion | flops 80805888 | bytes 2675204 | tf_op jit(solution)/shard_map/while/body/eval_jaxpr/dot_general | solution.py:93
  117.5 3.1 %fusion.38 = f32[16,768,64]{1,2,0:T(8,128)} fusion(f32[16,768,64]{1,2,0:T(8,128)} %get-tuple-element.299, s32[]{:T(128)} %get-tuple-element.298, f32[1,768,768]{2,1,0:T(8,128)} %get-tuple-element.311, s32[768]{0:T(1024)S(1)} %get-tuple-element.316, f32[768]{0:T(1024)S(1)} %get-tuple-element.261, f32[768]{0:T(1024)S(1)} %get-tuple-element.262, ...), kind=kOutput, calls=%fused_computation.11.clone.1 | convolution fusion | flops 80805888 | bytes 2675204 | tf_op jit(solution)/shard_map/while/body/eval_jaxpr/dot_general | solution.py:93
  123.3 3.1 %fusion.38 = f32[16,768,64]{1,2,0:T(8,128)} fusion(f32[16,768,64]{1,2,0:T(8,128)} %get-tuple-element.299, s32[]{:T(128)} %get-tuple-element.298, f32[1,768,768]{2,1,0:T(8,128)} %get-tuple-element.311, s32[768]{0:T(1024)S(1)} %get-tuple-element.316, f32[768]{0:T(1024)S(1)} %get-tuple-element.261, f32[768]{0:T(1024)S(1)} %get-tuple-element.262, ...), kind=kOutput, calls=%fused_computation.11.clone.1 | convolution fusion | flops 80805888 | bytes 2675204 | tf_op jit(solution)/shard_map/while/body/eval_jaxpr/dot_general | solution.py:93
  129.1 3.1 %fusion.38 = f32[16,768,64]{1,2,0:T(8,128)} fusion(f32[16,768,64]{1,2,0:T(8,128)} %get-tuple-element.299, s32[]{:T(128)} %get-tuple-element.298, f32[1,768,768]{2,1,0:T(8,128)} %get-tuple-element.311, s32[768]{0:T(1024)S(1)} %get-tuple-element.316, f32[768]{0:T(1024)S(1)} %get-tuple-element.261, f32[768]{0:T(1024)S(1)} %get-tuple-element.262, ...), kind=kOutput, calls=%fused_computation.11.clone.1 | convolution fusion | flops 80805888 | bytes 2675204 | tf_op jit(solution)/shard_map/while/body/eval_jaxpr/dot_general | solution.py:93
  135.0 3.1 %fusion.38 = f32[16,768,64]{1,2,0:T(8,128)} fusion(f32[16,768,64]{1,2,0:T(8,128)} %get-tuple-element.299, s32[]{:T(128)} %get-tuple-element.298, f32[1,768,768]{2,1,0:T(8,128)} %get-tuple-element.311, s32[768]{0:T(1024)S(1)} %get-tuple-element.316, f32[768]{0:T(1024)S(1)} %get-tuple-element.261, f32[768]{0:T(1024)S(1)} %get-tuple-element.262, ...), kind=kOutput, calls=%fused_computation.11.clone.1 | convolution fusion | flops 80805888 | bytes 2675204 | tf_op jit(solution)/shard_map/while/body/eval_jaxpr/dot_general | solution.py:93
  140.8 3.1 %fusion.38 = f32[16,768,64]{1,2,0:T(8,128)} fusion(f32[16,768,64]{1,2,0:T(8,128)} %get-tuple-element.299, s32[]{:T(128)} %get-tuple-element.298, f32[1,768,768]{2,1,0:T(8,128)} %get-tuple-element.311, s32[768]{0:T(1024)S(1)} %get-tuple-element.316, f32[768]{0:T(1024)S(1)} %get-tuple-element.261, f32[768]{0:T(1024)S(1)} %get-tuple-element.262, ...), kind=kOutput, calls=%fused_computation.11.clone.1 | convolution fusion | flops 80805888 | bytes 2675204 | tf_op jit(solution)/shard_map/while/body/eval_jaxpr/dot_general | solution.py:93
  158.3 3.1 %fusion.38 = f32[16,768,64]{1,2,0:T(8,128)} fusion(f32[16,768,64]{1,2,0:T(8,128)} %get-tuple-element.299, s32[]{:T(128)} %get-tuple-element.298, f32[1,768,768]{2,1,0:T(8,128)} %get-tuple-element.311, s32[768]{0:T(1024)S(1)} %get-tuple-element.316, f32[768]{0:T(1024)S(1)} %get-tuple-element.261, f32[768]{0:T(1024)S(1)} %get-tuple-element.262, ...), kind=kOutput, calls=%fused_computation.11.clone.1 | convolution fusion | flops 80805888 | bytes 2675204 | tf_op jit(solution)/shard_map/while/body/eval_jaxpr/dot_general | solution.py:93
  164.1 3.1 %fusion.38 = f32[16,768,64]{1,2,0:T(8,128)} fusion(f32[16,768,64]{1,2,0:T(8,128)} %get-tuple-element.299, s32[]{:T(128)} %get-tuple-element.298, f32[1,768,768]{2,1,0:T(8,128)} %get-tuple-element.311, s32[768]{0:T(1024)S(1)} %get-tuple-element.316, f32[768]{0:T(1024)S(1)} %get-tuple-element.261, f32[768]{0:T(1024)S(1)} %get-tuple-element.262, ...), kind=kOutput, calls=%fused_computation.11.clone.1 | convolution fusion | flops 80805888 | bytes 2675204 | tf_op jit(solution)/shard_map/while/body/eval_jaxpr/dot_general | solution.py:93
  167.3 18.6 %while.23 = (s32[]{:T(128)}, f32[16,64,128]{2,1,0:T(8,128)S(1)}, s32[]{:T(128)}, f32[16,16]{1,0:T(8,128)S(1)}, f32[16,16,64,128]{3,2,1,0:T(8,128)}, /*index=5*/s32[]{:T(128)}, s32[]{:T(128)}, s32[]{:T(128)}) while((s32[]{:T(128)}, f32[16,64,128]{2,1,0:T(8,128)S(1)}, s32[]{:T(128)}, f32[16,16]{1,0:T(8,128)S(1)}, f32[16,16,64,128]{3,2,1,0:T(8,128)}, ...), condition=%wide.region_5.6_spmd, body=%wide.region_4.5_spmd.sunk | while | flops 262149 | bytes 1573183 | solution.py:26
  185.9 6.2 %multiply_reduce_fusion = (f32[768]{0:T(1024)S(1)}, f32[768,16,64]{0,2,1:T(8,128)}) fusion(f32[768,16,64]{0,2,1:T(8,128)} %bitcast.146, bf16[768,16,64]{0,2,1:T(8,128)(2,1)S(1)} %get-tuple-element.321, f32[16]{0:T(128)S(1)} %bitcast.168, f32[16,64,128]{2,1,0:T(8,128)S(1)} %get-tuple-element.92, bf16[768,128]{1,0:T(8,128)(2,1)S(1)} %bitcast.167, ...), kind=kOutput, calls=%fused_computation.24 | convolution fusion | flops 1220148480 | bytes 11788352 | tf_op jit(solution)/shard_map/tgn,gkpn->tgkp/dot_general | solution.py:116
  192.2 5.8 %reshape.267 = f32[4,192,1024]{1,0,2:T(4,128)} reshape(f32[768,16,64]{0,2,1:T(8,128)} %get-tuple-element.177) | data formatting | bytes 6291456 | tf_op jit(solution)/shard_map/reshape | solution.py:128
  197.9 3.5 %copy.49 = f32[4,192,1024]{2,1,0:T(8,128)S(1)} copy(f32[4,192,1024]{1,0,2:T(4,128)} %reshape.267) | data formatting | bytes 6291456 | tf_op jit(solution)/shard_map/reshape | solution.py:128
  204.5 18.9 %all_to_all.16 = bf16[4,192,1024]{2,1,0:T(8,128)(2,1)S(1)} all-to-all(bf16[4,192,1024]{2,1,0:T(8,128)(2,1)S(1)} %multiply_convert_fusion), channel_id=1, replica_groups=mesh['pipe'=8,'ctx'=16,'head'=4] {'head'}, dimensions={0} | all-to-all | bytes 3145728 | tf_op jit(solution)/shard_map/all_to_all | solution.py:135
  223.6 21.0 %collective-permute-done.4 = bf16[192,4096]{1,0:T(8,128)(2,1)S(1)} collective-permute-done((bf16[192,4096]{1,0:T(8,128)(2,1)S(1)}, bf16[192,4096]{1,0:T(8,128)(2,1)S(1)}, u32[]{:S(2)}, u32[]{:S(2)}) %collective-permute-start.4) | collective-permute-done | bytes 1572896 | tf_op jit(solution)/shard_map/ppermute | solution.py:32
  (175 shorter events, 65.6 us)
Async XLA Ops:
  6.5 9.1 %copy-start.1 = (f32[1,768,16]{1,2,0:T(8,128)S(1)}, f32[1,768,16]{1,2,0:T(8,128)}, u32[]{:S(2)}) copy-start(f32[1,768,16]{1,2,0:T(8,128)} %param.20) | copy-start | bytes 147460
  6.5 11.2 %copy-start.4 = (f32[1,4,1024]{2,1,0:T(4,128)S(1)}, f32[1,4,1024]{2,1,0:T(4,128)}, u32[]{:S(2)}) copy-start(f32[1,4,1024]{2,1,0:T(4,128)} %param.22) | copy-start | bytes 49156
  6.6 160.7 %all-gather.4.cloned.1.call-start = ((), (), s32[]{:S(2)}) async-start(), calls=%async_computation.1 | async-start | bytes 8912896 | tf_op jit(solution)/shard_map/all_gather | solution.py:18
  7.4 11.0 %collective-permute-start = (s32[3]{0:T(128)S(1)}, s32[3]{0:T(128)S(1)}, u32[]{:S(2)}, u32[]{:S(2)}) collective-permute-start(s32[3]{0:T(128)S(1)} %slice_bitcast_fusion.11), channel_id=1, source_target_pairs={{0,4},{4,8},{8,12},{12,16},{16,20},{20,24},{24,28},{28,32},{32,36}... | collective-permute-start | bytes 44 | tf_op jit(solution)/shard_map/ppermute | solution.py:13
  9.9 18.9 %collective-permute-start.2 = (bf16[3,128]{1,0:T(4,128)(2,1)}, bf16[3,128]{1,0:T(4,128)(2,1)}, u32[]{:S(2)}, u32[]{:S(2)}) collective-permute-start(bf16[3,128]{1,0:T(4,128)(2,1)} %slice_bitcast_fusion.1), channel_id=1, source_target_pairs={{0,4},{4,8},{8,12},{12,16},{16,20},{20,24},{24,28},{28,32},{32,36}... | collective-permute-start | bytes 2312 | tf_op jit(solution)/shard_map/ppermute | solution.py:13
  13.0 11.2 %collective-permute-start.3 = (bf16[3,1024]{0,1:T(8,128)(2,1)S(1)}, bf16[3,1024]{0,1:T(8,128)(2,1)S(1)}, u32[]{:S(2)}, u32[]{:S(2)}) collective-permute-start(bf16[3,1024]{0,1:T(8,128)(2,1)S(1)} %slice_bitcast_fusion), channel_id=1, source_target_pairs={{0,4},{4,8},{8,12},{12,16},{16,20},{20,24},{24,28},{28,32},{32,36}... | collective-permute-start | bytes 18440 | tf_op jit(solution)/shard_map/ppermute | solution.py:13
  15.0 9.2 %copy-start.2 = (s32[768]{0:T(1024)}, s32[768]{0:T(1024)S(1)}, u32[]{:S(2)}) copy-start(s32[768]{0:T(1024)S(1)} %reduce.3) | copy-start | bytes 9220
  32.5 36.7 %collective-permute-start.1 = (bf16[3,128]{1,0:T(4,128)(2,1)S(1)}, bf16[3,128]{1,0:T(4,128)(2,1)S(1)}, u32[]{:S(2)}, u32[]{:S(2)}) collective-permute-start(bf16[3,128]{1,0:T(4,128)(2,1)S(1)} %slice_bitcast_fusion.2), channel_id=1, source_target_pairs={{0,4},{4,8},{8,12},{12,16},{16,20},{20,24},{24,28},{28,32},{32,36}... | collective-permute-start | bytes 2312 | tf_op jit(solution)/shard_map/ppermute | solution.py:13
  35.9 33.8 %copy-start.7 = (pred[768]{0:T(1024)(128)(4,1)S(1)}, pred[768]{0:T(1024)(128)(4,1)}, u32[]{:S(2)}) copy-start(pred[768]{0:T(1024)(128)(4,1)} %get-tuple-element.165) | copy-start | bytes 2308
  35.9 33.8 %copy-start.9 = (pred[768]{0:T(1024)(128)(4,1)S(1)}, pred[768]{0:T(1024)(128)(4,1)}, u32[]{:S(2)}) copy-start(pred[768]{0:T(1024)(128)(4,1)} %get-tuple-element.166) | copy-start | bytes 2308
  35.9 33.8 %copy-start.11 = (pred[768]{0:T(1024)(128)(4,1)S(1)}, pred[768]{0:T(1024)(128)(4,1)}, u32[]{:S(2)}) copy-start(pred[768]{0:T(1024)(128)(4,1)} %get-tuple-element.167) | copy-start | bytes 2308
  35.9 33.8 %copy-start.17 = (f32[128]{0:T(128)S(1)}, f32[128]{0:T(128)}, u32[]{:S(2)}) copy-start(f32[128]{0:T(128)} %get-tuple-element.170) | copy-start | bytes 1540
  35.9 33.8 %copy-start.18 = (f32[128]{0:T(128)S(1)}, f32[128]{0:T(128)}, u32[]{:S(2)}) copy-start(f32[128]{0:T(128)} %get-tuple-element.171) | copy-start | bytes 1540
  36.0 33.8 %copy-start.19 = (f32[128]{0:T(128)S(1)}, f32[128]{0:T(128)}, u32[]{:S(2)}) copy-start(f32[128]{0:T(128)} %get-tuple-element.172) | copy-start | bytes 1540
  36.0 33.8 %copy-start.20 = (f32[128]{0:T(128)S(1)}, f32[128]{0:T(128)}, u32[]{:S(2)}) copy-start(f32[128]{0:T(128)} %get-tuple-element.173) | copy-start | bytes 1540
  36.0 33.8 %copy-start.22 = (f32[128]{0:T(128)S(1)}, f32[128]{0:T(128)}, u32[]{:S(2)}) copy-start(f32[128]{0:T(128)} %get-tuple-element.168) | copy-start | bytes 1540
  36.0 33.8 %copy-start.24 = (f32[128]{0:T(128)S(1)}, f32[128]{0:T(128)}, u32[]{:S(2)}) copy-start(f32[128]{0:T(128)} %get-tuple-element.169) | copy-start | bytes 1540
  36.0 33.8 %copy-start.26 = (f32[128]{0:T(128)S(1)}, f32[128]{0:T(128)}, u32[]{:S(2)}) copy-start(f32[128]{0:T(128)} %get-tuple-element.174) | copy-start | bytes 1540
  36.0 33.8 %copy-start.28 = (f32[128]{0:T(128)S(1)}, f32[128]{0:T(128)}, u32[]{:S(2)}) copy-start(f32[128]{0:T(128)} %get-tuple-element.175) | copy-start | bytes 1540
  36.0 33.8 %copy-start.29 = (bf16[1,768,128]{2,1,0:T(8,128)(2,1)S(1)}, bf16[1,768,128]{2,1,0:T(8,128)(2,1)}, u32[]{:S(2)}) copy-start(bf16[1,768,128]{2,1,0:T(8,128)(2,1)} %param.17) | copy-start | bytes 589828
  167.3 18.6 %copy-start.30 = (bf16[1,768,128]{2,1,0:T(8,128)(2,1)S(1)}, bf16[1,768,128]{2,1,0:T(8,128)(2,1)}, u32[]{:S(2)}) copy-start(bf16[1,768,128]{2,1,0:T(8,128)(2,1)} %param.18) | copy-start | bytes 589828
  167.3 18.6 %copy-start.32 = (bf16[3,128]{1,0:T(4,128)(2,1)S(1)}, bf16[3,128]{1,0:T(4,128)(2,1)}, u32[]{:S(2)}) copy-start(bf16[3,128]{1,0:T(4,128)(2,1)} %copy-done.31) | copy-start | bytes 2308
  167.3 18.6 %copy-start.33 = (f32[1,16]{1,0:T(1,128)S(1)}, f32[1,16]{1,0:T(1,128)}, u32[]{:S(2)}) copy-start(f32[1,16]{1,0:T(1,128)} %param.26) | copy-start | bytes 196
  223.5 21.1 %collective-permute-start.4 = (bf16[192,4096]{1,0:T(8,128)(2,1)S(1)}, bf16[192,4096]{1,0:T(8,128)(2,1)S(1)}, u32[]{:S(2)}, u32[]{:S(2)}) collective-permute-start(bf16[192,4096]{1,0:T(8,128)(2,1)S(1)} %bitcast.149), channel_id=1, source_target_pairs={{0,64},{64,128},{128,192},{192,256},{256,320},{320,384},{384,448},... | collective-permute-start | bytes 4718600 | tf_op jit(solution)/shard_map/ppermute | solution.py:32
  (16 other events, 95.0 us)
Sparse Core Ops, SparseCore 0:
  31.9 106.2 all-gather.3
where the time goes:
time: 255 us; the launch traced here: 253 us
  matrix products  62.4 us (24%)
  blocking collectives  49.9 us (20%)
  loops' own time  33.8 us (13%)
  other arithmetic  32.2 us (13%)
  local copies, waits for them, and re-layouts  31.9 us (13%)
  waiting for transfers between devices  22.1 us (9%)
  between operations  15.2 us (6%)
  starting transfers between devices  5.19 us (2%)
    dot_general x16, matrix products, one_head(): return jnp.dot(weights, x_head, preferred_element_type=jnp.float32)  49.3 us
    another operation x1, loops' own time, shards(): intra = lax.map(one_head, jnp.arange(heads_local))  33.2 us
    all_gather x1, blocking collectives, carried_in(): gathered = jax.tree.map(lambda a: lax.all_gather(a, axis), part)  31.1 us
    ppermute x1, waiting for transfers between devices, shifted(): return lax.ppermute(value, axis, pairs)  21 us
    all_to_all x1, blocking collectives, shards(): lax.all_to_all(section_out, 'head', split_axis=0, concat_axis=1, tiled=True)  18.9 us
    add x15, other arithmetic, link(): later[0][:, None, None] * earlier[1] + later[1]  17.8 us
    dynamic_slice x16, local copies, waits for them, and re-layouts, shards(): intra = lax.map(one_head, jnp.arange(heads_local))  10.6 us
    reshape x2, local copies, waits for them, and re-layouts, shards(): mixed.reshape(length, heads_local * head_width)  9.31 us
  transfers between devices with their start and end apart: 6, of which 2 were waited for; matrix products, arithmetic and copies ran while one was open for 33% of the time, Pallas kernels for 0%

commit v1 on v0

v1 whole, which is shorter than its diff:
```python
import functools

import jax
import jax.numpy as jnp
from jax import lax
from jax.experimental import pallas as pl
from jax.experimental.pallas import tpu as pltpu
from jax.sharding import PartitionSpec as P

F32 = jnp.float32
BF16 = jnp.bfloat16
MESH = pl.DeviceIdType.MESH
CHUNK = 256
LANES = 128
MARGIN = 16
GROUP = 4
HI = lax.Precision.HIGHEST


def nt(a, b, **kw):
    return lax.dot_general(a, b, (((1,), (1,)), ((), ())), preferred_element_type=F32, **kw)


def nn(a, b, **kw):
    return lax.dot_general(a, b, (((1,), (0,)), ((), ())), preferred_element_type=F32, **kw)


def halves(a):
    high = a.astype(BF16)
    return high, (a - high.astype(F32)).astype(BF16)


def silu(a):
    half = 0.5 * a
    return half + half * jnp.tanh(half)


def column(row):
    return jnp.broadcast_to(row, (LANES, LANES)).T


def kernel(
    sizes,
    x_hbm, b_hbm, c_hbm, z_hbm, dt_ref, seg_hbm, conv_x, conv_bc, rate_ref, bias_ref, skip_ref, gain_ref,
    out_hbm,
    xv, bv, cv, zv, segv, mx, mb, mc, mseg, ext, segc, taps, fin, fout, ent, spread, rows_s, bmt, smask, cs, cmask,
    xs, xsc, hid, yg, eg, ssq, chain_in, chain_out, exch_in, relay_in, relay_out, sendbuf, recvbuf, scale_out, scale_in,
    stage,
    load_sem, marg_send, marg_recv, ch_send, ch_recv, ex_send, ex_recv, re_send, re_recv, o_send, o_recv, s_send, s_recv,
    out_sem,
):
    n_pipe, n_ctx, n_head = sizes
    tokens, width = x_hbm.shape
    pieces, chunks = width // LANES, tokens // CHUNK
    heads = rate_ref.shape[1]
    share = tokens // n_head
    sec, blk, me = lax.axis_index("pipe"), lax.axis_index("ctx"), lax.axis_index("head")
    group, place = blk // GROUP, lax.rem(blk, GROUP)
    dest_sec = lax.rem(sec + 1, n_pipe)

    loads = []
    for p in range(pieces):
        loads.append(pltpu.make_async_copy(x_hbm.at[:, pl.ds(p * LANES, LANES)], xv.at[p], load_sem.at[p]))
    for n, (src, dst) in enumerate(((b_hbm, bv), (c_hbm, cv), (z_hbm, zv), (seg_hbm, segv))):
        loads.append(pltpu.make_async_copy(src, dst, load_sem.at[pieces + n]))
    for copy in reversed(loads):
        copy.start()

    barrier = pltpu.get_barrier_semaphore()
    count = 0
    for step in (1, GROUP):
        for peer in (blk + step, blk + n_ctx - step):
            pl.semaphore_signal(barrier, inc=1, device_id={"ctx": lax.rem(peer, n_ctx)}, device_id_type=MESH)
            count += 1
    for peer in (dest_sec, lax.rem(sec + n_pipe - 1, n_pipe)):
        for h in range(n_head):
            pl.semaphore_signal(barrier, inc=1, device_id={"pipe": peer, "head": h}, device_id_type=MESH)
            count += 1
    pl.semaphore_wait(barrier, count)

    nxt = {"ctx": lax.rem(blk + 1, n_ctx)}
    far = {"ctx": lax.rem(blk + GROUP, n_ctx)}

    def remote(src, dst, send, recv, device):
        return pltpu.make_async_remote_copy(
            src_ref=src, dst_ref=dst, send_sem=send, recv_sem=recv, device_id=device, device_id_type=MESH
        )

    margins = [
        remote(b_hbm.at[pl.ds(tokens - MARGIN, MARGIN), :], mb, marg_send.at[0], marg_recv.at[0], nxt),
        remote(c_hbm.at[pl.ds(tokens - MARGIN, MARGIN), :], mc, marg_send.at[1], marg_recv.at[1], nxt),
        remote(seg_hbm.at[:, pl.ds(tokens - LANES, LANES)], mseg, marg_send.at[2], marg_recv.at[2], nxt),
        remote(x_hbm.at[pl.ds(tokens - MARGIN, MARGIN), :], mx, marg_send.at[3], marg_recv.at[3], nxt),
    ]

    @pl.when(blk < n_ctx - 1)
    def _():
        for copy in margins:
            copy.start()

    def chain_copy(p):
        return remote(chain_out.at[p], chain_in.at[p], ch_send.at[p], ch_recv.at[p], nxt)

    def exch_copy(p):
        return remote(chain_in.at[p, pl.ds(0, LANES), :], exch_in.at[p], ex_send.at[p], ex_recv.at[p], far)

    def relay_copy(p):
        return remote(relay_out.at[p], relay_in.at[p], re_send.at[p], re_recv.at[p], nxt)

    def relay_on(p):
        return remote(relay_in.at[p], relay_in.at[p], re_send.at[p], re_recv.at[p], nxt)

    def row_copy(p, d):
        return remote(
            sendbuf.at[p, pl.ds(d * share, share), :],
            recvbuf.at[me, p],
            o_send.at[d, p],
            o_recv.at[me, p],
            {"pipe": dest_sec, "head": d},
        )

    def row_wait(p, h):
        remote(
            sendbuf.at[p, pl.ds(0, share), :], recvbuf.at[h, p], o_send.at[0, p], o_recv.at[h, p],
            {"pipe": dest_sec, "head": 0},
        ).wait_recv()

    def scale_copy(d):
        return remote(scale_out.at[d], scale_in.at[me], s_send.at[d], s_recv.at[me], {"pipe": dest_sec, "head": d})

    def scale_wait(h):
        remote(
            scale_out.at[0], scale_in.at[h], s_send.at[0], s_recv.at[h], {"pipe": dest_sec, "head": 0}
        ).wait_recv()

    loads[pieces + 3].wait()
    eye = lax.broadcasted_iota(jnp.int32, (heads, heads), 0) == lax.broadcasted_iota(jnp.int32, (heads, heads), 1)
    bias = jnp.sum(jnp.where(eye, bias_ref[...], 0.0), axis=1, keepdims=True)
    rate = jnp.sum(jnp.where(eye, rate_ref[...], 0.0), axis=1, keepdims=True)
    raw = dt_ref[...] + bias
    steps = jnp.maximum(raw, 0.0) + jnp.log1p(jnp.exp(-jnp.abs(raw)))
    decay = -steps * rate
    at = lax.broadcasted_iota(jnp.int32, (CHUNK, CHUNK), 0)
    of = lax.broadcasted_iota(jnp.int32, (CHUNK, CHUNK), 1)
    lower = (at >= of).astype(F32)
    unit = (at == of).astype(F32)
    for p in range(pieces):
        head_of = lax.broadcasted_iota(jnp.int32, (heads, LANES), 0)
        lane = lax.broadcasted_iota(jnp.int32, (heads, LANES), 1)
        spread[p] = (head_of == p * (heads // pieces) + lane // (LANES // (heads // pieces))).astype(BF16)

    for n in range(tokens // LANES):
        segc[pl.ds(MARGIN + n * LANES, LANES), :] = column(segv[:, pl.ds(n * LANES, LANES)].astype(F32))

    @pl.when(blk == 0)
    def _():
        mx[...] = jnp.zeros_like(mx)
        mb[...] = jnp.zeros_like(mb)
        mc[...] = jnp.zeros_like(mc)
        mseg[...] = jnp.full_like(mseg, -1)

    @pl.when(blk > 0)
    def _():
        for copy in margins[:3]:
            copy.wait_recv()

    segc[pl.ds(0, MARGIN), :] = column(mseg[...].astype(F32))[LANES - MARGIN :, :]
    for j in range(1, 4):
        for r in range(0, tokens, LANES):
            same = segc[pl.ds(MARGIN + r - j, LANES), :] == segc[pl.ds(MARGIN + r, LANES), :]
            taps[j - 1, pl.ds(r, LANES), :] = same.astype(F32)
    prior = segc[pl.ds(MARGIN - 1, 1), :]
    lasts = [segc[pl.ds(MARGIN + (j + 1) * CHUNK - 1, 1), :] for j in range(chunks)]

    base = jnp.zeros((1, heads), F32)
    rows = []
    for j in range(chunks):
        span = pl.ds(j * CHUNK, CHUNK)
        cum = nt(lower, decay[:, j * CHUNK : (j + 1) * CHUNK], precision=HI)
        step = nt(unit, steps[:, j * CHUNK : (j + 1) * CHUNK], precision=HI)
        last_cum = cum[CHUNK - 1 :, :]
        fin[0, span, :], fin[1, span, :] = halves(jnp.exp(-cum) * step)
        fout[0, span, :], fout[1, span, :] = halves(jnp.exp(cum))
        here = segc[pl.ds(MARGIN + j * CHUNK, CHUNK), :][:, :heads] == prior[:, :heads]
        ent[0, span, :], ent[1, span, :] = halves(jnp.where(here, jnp.exp(cum + base), 0.0))
        base = base + last_cum
        rows.append(jnp.exp(last_cum))
        if j > 0:
            rows.append(jnp.where((lasts[j] == lasts[j - 1])[:, :heads], rows[-1], 0.0))
    rows.append(jnp.where((lasts[-1] == prior)[:, :heads], jnp.exp(base), 0.0))
    rows.append(skip_ref[...])
    rows.append(jnp.zeros((16 - len(rows), heads), F32))
    rows_s[0], rows_s[1] = halves(jnp.concatenate(rows, axis=0))

    def convolved(get, put):
        pass

    def conv_rows(w, r, size):
        total = w[3:4, :] * ext[pl.ds(MARGIN + r, size), :]
        for j in range(1, 4):
            shifted = ext[pl.ds(MARGIN + r - j, size), :]
            total = total + (w[3 - j : 4 - j, :] * shifted) * taps[j - 1, pl.ds(r, size), :]
        return silu(total)

    part = 64
    loads[pieces].wait()
    ext[pl.ds(0, MARGIN), :] = mb[...].astype(F32)
    ext[pl.ds(MARGIN, tokens), :] = bv[...].astype(F32)
    for r in range(0, tokens, part):
        bv[pl.ds(r, part), :] = conv_rows(conv_bc[0], r, part).astype(BF16)
    loads[pieces + 1].wait()
    ext[pl.ds(0, MARGIN), :] = mc[...].astype(F32)
    ext[pl.ds(MARGIN, tokens), :] = cv[...].astype(F32)
    for r in range(0, tokens, part):
        cs[pl.ds(r, part), :] = conv_rows(conv_bc[1], r, part).astype(BF16)
    for j in range(chunks):
        seg_t = segc[pl.ds(MARGIN + j * CHUNK, CHUNK), :]
        state_in = bv[pl.ds(j * CHUNK, CHUNK), :]
        kept = jnp.where(seg_t == lasts[j], state_in.astype(F32), 0.0)
        bmt[j] = kept.T.astype(BF16)

    @pl.when(blk > 0)
    def _():
        margins[3].wait_recv()

    def expand(pair, span, p):
        return nn(pair[0, span, :], spread[p]) + nn(pair[1, span, :], spread[p])

    @pl.loop(0, pieces)
    def _(p):
        lanes = pl.ds(pl.multiple_of(p * LANES, LANES), LANES)
        pltpu.make_async_copy(x_hbm.at[:, lanes], xv.at[p], load_sem.at[p]).wait()
        ext[pl.ds(0, MARGIN), :] = mx[:, lanes].astype(F32)
        ext[pl.ds(MARGIN, tokens), :] = xv[p].astype(F32)
        w = conv_x[:, lanes]
        factors = expand(rows_s, pl.ds(0, 16), p)
        state, row = None, 0
        for j in range(chunks):
            for r in range(j * CHUNK, (j + 1) * CHUNK, part):
                span = pl.ds(r, part)
                value = conv_rows(w, r, part).astype(BF16)
                xs[p, span, :] = value
                xsc[p, span, :] = (value.astype(F32) * expand(fin, span, p)).astype(BF16)
            own = nn(bmt[j], xsc[p, pl.ds(j * CHUNK, CHUNK), :])
            if j == 0:
                state = factors[row : row + 1, :] * own
                row += 1
            else:
                hid[p, j - 1] = state.astype(BF16)
                state = factors[row + 1 : row + 2, :] * state + factors[row : row + 1, :] * own
                row += 2
        through = factors[row : row + 1, :]

        @pl.when(place == 0)
        def _():
            chain_out[p, pl.ds(0, LANES), :] = state.astype(BF16)
            high, low = halves(through)
            chain_out[p, pl.ds(LANES, 16), :] = jnp.concatenate(
                [high, low, jnp.zeros((14, LANES), BF16)], axis=0
            )

        @pl.when(place > 0)
        def _():
            chain_copy(p).wait_recv()
            tail = chain_in[p, pl.ds(LANES, 16), :].astype(F32)
            so_far = tail[0:1, :] + tail[1:2, :]
            chain_out[p, pl.ds(0, LANES), :] = (
                state + through * chain_in[p, pl.ds(0, LANES), :].astype(F32)
            ).astype(BF16)
            high, low = halves(through * so_far)
            chain_out[p, pl.ds(LANES, 16), :] = jnp.concatenate(
                [high, low, jnp.zeros((14, LANES), BF16)], axis=0
            )

        @pl.when(blk < n_ctx - 1)
        def _():
            chain_copy(p).start()

    for j in range(chunks):
        span = pl.ds(j * CHUNK, CHUNK)
        seg_t = segc[pl.ds(MARGIN + j * CHUNK, CHUNK), :]
        for half in range(0, CHUNK, LANES):
            seg_u = segv[:, pl.ds(j * CHUNK + half, LANES)].astype(F32)
            score = nt(cs[span, :], bv[pl.ds(j * CHUNK + half, LANES), :])
            keep = (seg_t == seg_u) & (at[:, :LANES] >= of[:, :LANES] + half)
            smask[j, :, pl.ds(half, LANES)] = jnp.where(keep, score, 0.0).astype(BF16)
        if j > 0:
            kept = jnp.where(seg_t == lasts[j - 1], cs[span, :].astype(F32), 0.0)
            cmask[j - 1] = kept.astype(BF16)
    loads[pieces + 2].wait()

    @pl.loop(0, pieces)
    def _(p):
        lanes = pl.ds(pl.multiple_of(p * LANES, LANES), LANES)
        factors = expand(rows_s, pl.ds(0, 16), p)
        skip = factors[2 * chunks : 2 * chunks + 1, :]
        for j in range(chunks):
            inner = nn(smask[j], xsc[p, pl.ds(j * CHUNK, CHUNK), :])
            if j > 0:
                inner = inner + nn(cmask[j - 1], hid[p, j - 1])
            for r in range(0, CHUNK, part):
                span = pl.ds(j * CHUNK + r, part)
                gate = silu(zv[span, lanes].astype(F32))
                mixed = expand(fout, span, p) * inner[r : r + part, :] + skip * xs[p, span, :].astype(F32)
                yg[p, span, :] = mixed * gate
                eg[p, span, :] = expand(ent, span, p) * gate

        @pl.when((place == 0) & (group > 0))
        def _():
            chain_copy(p).wait_recv()

        @pl.when((place == 0) & (group > 0) & (blk + GROUP < n_ctx))
        def _():
            exch_copy(p).start()

    ssq[...] = jnp.zeros_like(ssq)
    scale_out[...] = jnp.zeros_like(scale_out)

    @pl.loop(0, pieces)
    def _(p):
        lanes = pl.ds(pl.multiple_of(p * LANES, LANES), LANES)

        @pl.when(blk == 0)
        def _():
            relay_out[p] = jnp.zeros((LANES, LANES), BF16)

        @pl.when((place == 0) & (group == 1))
        def _():
            relay_out[p] = chain_in[p, pl.ds(0, LANES), :]

        @pl.when((place == 0) & (group > 1))
        def _():
            exch_copy(p).wait_recv()
            tail = chain_in[p, pl.ds(LANES, 16), :].astype(F32)
            so_far = tail[0:1, :] + tail[1:2, :]
            relay_out[p] = (
                chain_in[p, pl.ds(0, LANES), :].astype(F32) + so_far * exch_in[p].astype(F32)
            ).astype(BF16)

        @pl.when((place == 0) & (group > 0))
        def _():
            relay_copy(p).start()

        @pl.when((place > 0) & (group == 0))
        def _():
            relay_out[p] = chain_in[p, pl.ds(0, LANES), :]

        @pl.when((place > 0) & (group > 0))
        def _():
            relay_on(p).wait_recv()

        @pl.when((place > 0) & (place < GROUP - 1) & (group > 0))
        def _():
            relay_on(p).start()

        @pl.when((place > 0) & (group > 0))
        def _():
            tail = chain_in[p, pl.ds(LANES, 16), :].astype(F32)
            so_far = tail[0:1, :] + tail[1:2, :]
            relay_out[p] = (
                chain_in[p, pl.ds(0, LANES), :].astype(F32) + so_far * relay_in[p].astype(F32)
            ).astype(BF16)

        gain = gain_ref[:, lanes]
        for r in range(0, tokens, part):
            span = pl.ds(r, part)
            gated = yg[p, span, :] + eg[p, span, :] * nn(cs[span, :], relay_out[p])
            ssq[span, :] += gated * gated
            sendbuf[p, span, :] = (gated * gain).astype(BF16)
        for turn in range(n_head):
            row_copy(p, lax.rem(me + turn, n_head)).start()

    for d in range(n_head):
        for n, first in enumerate((0, share - LANES)):
            total = jnp.sum(ssq[pl.ds(d * share + first, LANES), :].T, axis=0, keepdims=True)
            scale_out[d, pl.ds(n, 1), :] = lax.rsqrt(total * (1.0 / width) + 1e-05)
        scale_copy(d).start()

    for h in range(n_head):
        scale_wait(h)
        first = column(scale_in[h, pl.ds(0, 1), :])
        second = column(scale_in[h, pl.ds(1, 1), :])

        @pl.loop(0, pieces)
        def _(p):
            row_wait(p, h)
            lanes = pl.ds(pl.multiple_of(h * width + p * LANES, LANES), LANES)
            stage[pl.ds(0, LANES), lanes] = (recvbuf[h, p, pl.ds(0, LANES), :].astype(F32) * first).astype(BF16)
            rest = share - LANES
            stage[pl.ds(LANES, rest), lanes] = (
                recvbuf[h, p, pl.ds(LANES, rest), :].astype(F32) * second[LANES - rest :, :]
            ).astype(BF16)

        pltpu.make_async_copy(
            stage.at[:, pl.ds(h * width, width)], out_hbm.at[:, pl.ds(h * width, width)], out_sem.at[h]
        ).start()

    for h in range(n_head):
        pltpu.make_async_copy(
            stage.at[:, pl.ds(h * width, width)], out_hbm.at[:, pl.ds(h * width, width)], out_sem.at[h]
        ).wait()
    for d in range(n_head):
        scale_copy(d).wait_send()

    @pl.loop(0, pieces)
    def _(p):
        for d in range(n_head):
            row_copy(p, d).wait_send()

        @pl.when(blk < n_ctx - 1)
        def _():
            chain_copy(p).wait_send()

        @pl.when((place == 0) & (group > 0) & (blk + GROUP < n_ctx))
        def _():
            exch_copy(p).wait_send()

        @pl.when((place < GROUP - 1) & (group > 0))
        def _():
            relay_copy(p).wait_send()

    @pl.when(blk < n_ctx - 1)
    def _():
        for copy in margins:
            copy.wait_send()


def solution(mesh):
    sizes = tuple(mesh.shape[name] for name in ("pipe", "ctx", "head"))
    n_head = sizes[2]

    def shards(
        x_in, b_in, c_in, z_in, dt_raw, seg_ids, conv_x, conv_bc, decay_rate, dt_bias, skip_d, norm_gain
    ):
        _, tokens, width = x_in.shape
        state = b_in.shape[2]
        heads = decay_rate.shape[1]
        pieces, chunks, share = width // LANES, tokens // CHUNK, tokens // n_head
        vmem, sem = pltpu.VMEM, pltpu.SemaphoreType.DMA
        scratch = [
            vmem((pieces, tokens, LANES), BF16),
            vmem((tokens, state), BF16),
            vmem((tokens, state), BF16),
            vmem((tokens, width), BF16),
            vmem((1, tokens), jnp.int32),
            vmem((MARGIN, width), BF16),
            vmem((MARGIN, state), BF16),
            vmem((MARGIN, state), BF16),
            vmem((1, LANES), jnp.int32),
            vmem((MARGIN + tokens, LANES), F32),
            vmem((MARGIN + tokens, LANES), F32),
            vmem((3, tokens, LANES), F32),
            vmem((2, tokens, heads), BF16),
            vmem((2, tokens, heads), BF16),
            vmem((2, tokens, heads), BF16),
            vmem((pieces, heads, LANES), BF16),
            vmem((2, 16, heads), BF16),
            vmem((chunks, state, CHUNK), BF16),
            vmem((chunks, CHUNK, CHUNK), BF16),
            vmem((tokens, state), BF16),
            vmem((chunks - 1, CHUNK, state), BF16),
            vmem((pieces, tokens, LANES), BF16),
            vmem((pieces, tokens, LANES), BF16),
            vmem((pieces, chunks - 1, state, LANES), BF16),
            vmem((pieces, tokens, LANES), F32),
            vmem((pieces, tokens, LANES), F32),
            vmem((tokens, LANES), F32),
            vmem((pieces, state + 16, LANES), BF16),
            vmem((pieces, state + 16, LANES), BF16),
            vmem((pieces, state, LANES), BF16),
            vmem((pieces, state, LANES), BF16),
            vmem((pieces, state, LANES), BF16),
            vmem((pieces, tokens, LANES), BF16),
            vmem((n_head, pieces, share, LANES), BF16),
            vmem((n_head, 8, LANES), F32),
            vmem((n_head, 8, LANES), F32),
            vmem((share, n_head * width), BF16),
            sem((pieces + 4,)),
            sem((4,)), sem((4,)),
            sem((pieces,)), sem((pieces,)),
            sem((pieces,)), sem((pieces,)),
            sem((pieces,)), sem((pieces,)),
            sem((n_head, pieces)), sem((n_head, pieces)),
            sem((n_head,)), sem((n_head,)),
            sem((n_head,)),
        ]
        anywhere = pl.BlockSpec(memory_space=pl.ANY)
        local = pl.BlockSpec(memory_space=pltpu.VMEM)
        rows = pl.pallas_call(
            functools.partial(kernel, sizes),
            out_shape=jax.ShapeDtypeStruct((share, n_head * width), BF16),
            in_specs=[anywhere] * 4 + [local, anywhere] + [local] * 6,
            out_specs=anywhere,
            scratch_shapes=scratch,
            compiler_params=pltpu.CompilerParams(collective_id=0, has_side_effects=True),
        )(
            x_in[0], b_in[0], c_in[0], z_in[0], dt_raw[0].T, seg_ids, conv_x[0], conv_bc[0],
            decay_rate, dt_bias, skip_d, norm_gain,
        )
        return rows[None]

    placed = (
        P("pipe", "ctx", "head"),
        P("pipe", "ctx", "head"),
        P("pipe", "ctx", "head"),
        P("pipe", "ctx", "head"),
        P("pipe", "ctx", "head"),
        P("pipe", "ctx"),
        P("pipe", None, "head"),
        P("pipe", None, None, "head"),
        P("pipe", "head"),
        P("pipe", "head"),
        P("pipe", "head"),
        P("pipe", "head"),
    )
    return jax.shard_map(
        shards,
        mesh=mesh,
        in_specs=placed,
        out_specs=P("pipe", ("ctx", "head"), None),
        check_vma=False,
    )
```

time: 255 us -> 65.5 us (0.26)
  the two profiles are of different devices: /device:TPU:480 before, /device:TPU:361 now
where the time goes in v1:
time: 65.5 us; the launch traced here: 65.3 us
  Pallas kernels  62.6 us (96%)
  local copies, waits for them, and re-layouts  2.7 us (4%)
    pallas_call x1, Pallas kernels, shards(): pl.pallas_call(functools.partial(kernel, sizes), out_shape=jax.ShapeDtype...  62.6 us
    unnamed x1, local copies, waits for them, and re-layouts  2.7 us

profile of v1, /device:TPU:361, one launch (start us, length us, event | category | flops | bytes accessed | tf_op | source)
XLA Modules:
  0.0 65.3 jit_solution(12220611838591178195)
XLA Ops:
  0.0 62.6 %shard_map.118 = bf16[192,4096]{1,0:T(8,128)(2,1)} custom-call(bf16[768,1024]{1,0:T(8,128)(2,1)} %bitcast.11, bf16[768,128]{1,0:T(8,128)(2,1)} %bitcast.13, bf16[768,128]{1,0:T(8,128)(2,1)} %bitcast.14, bf16[768,1024]{1,0:T(8,128)(2,1)} %bitcast.12, f32[16,768]{1,0:T(8,128)} %bitcast.15, s32[1,768]{1,0:T(1,128)} %seg_hbm.1, f32[4,1024]{1,0:T(4,128)} %bitcast.16, ...), custom_call_target="tpu_custom_call" | custom-call | tf_op jit(solution)/shard_map/pallas_call | solution.py:489
  62.6 2.7 %copy.14 = bf16[1,192,4096]{2,1,0:T(8,128)(2,1)} copy(bf16[1,192,4096]{2,1,0:T(8,128)(2,1)} %bitcast.10) | data formatting | bytes 3145728

commit v2 on v1

v2 whole, which is shorter than its diff:
```python
import functools

import jax
import jax.numpy as jnp
from jax import lax
from jax.experimental import pallas as pl
from jax.experimental.pallas import tpu as pltpu
from jax.sharding import PartitionSpec as P

F32 = jnp.float32
BF16 = jnp.bfloat16
MESH = pl.DeviceIdType.MESH
CHUNK = 256
LANES = 128
MARGIN = 16
HALF = 64


def nt(a, b, **kw):
    return lax.dot_general(a, b, (((1,), (1,)), ((), ())), preferred_element_type=F32, **kw)


def nn(a, b, **kw):
    return lax.dot_general(a, b, (((1,), (0,)), ((), ())), preferred_element_type=F32, **kw)


def halves(a):
    high = a.astype(BF16)
    return high, (a - high.astype(F32)).astype(BF16)


def silu(a):
    half = 0.5 * a
    return half + half * jnp.tanh(half)


def column(row):
    return jnp.broadcast_to(row, (LANES, LANES)).T


def kernel(
    sizes,
    x_hbm, b_hbm, c_hbm, z_hbm, dt_hbm, seg_hbm, convx_hbm, convbc_hbm, rate_hbm, bias_hbm, skip_hbm, gain_hbm,
    recvbuf, scale_in,
    xv, bv, cv, zv, dtv, segv, conv_x, conv_bc, ratev, biasv, skipv, gainv, mx, mb, mc, mseg,
    ext, segc, taps, fac, spread_in, spread_out, rows_s, bmt, smask, cs, cmask,
    xs, xsc, hid, yg, eg, ssq, loc_out, t_out, loc_in, t_in, scan_s, c_out, c_in, car, sendbuf, scale_out,
    load_sem, small_sem, marg_send, marg_recv, l_send, l_recv, t_send, t_recv, c_send, c_recv,
    o_send, o_recv, s_send, s_recv,
):
    n_pipe, n_ctx, n_head = sizes
    tokens, width = x_hbm.shape
    pieces, chunks = width // LANES, tokens // CHUNK
    heads = ratev.shape[1]
    share = tokens // n_head
    sec, blk, me = lax.axis_index("pipe"), lax.axis_index("ctx"), lax.axis_index("head")
    dest_sec = lax.rem(sec + 1, n_pipe)

    def ctx_of(step):
        return {"ctx": lax.rem(blk + n_ctx + step, n_ctx)}

    barrier = pltpu.get_barrier_semaphore()
    for step in range(1, n_ctx):
        pl.semaphore_signal(barrier, inc=1, device_id=ctx_of(step), device_id_type=MESH)
    for h in range(n_head):
        pl.semaphore_signal(
            barrier, inc=1, device_id={"pipe": lax.rem(sec + n_pipe - 1, n_pipe), "head": h}, device_id_type=MESH
        )

    smalls = [
        pltpu.make_async_copy(src, dst, small_sem.at[n])
        for n, (src, dst) in enumerate((
            (seg_hbm, segv), (dt_hbm, dtv), (bias_hbm, biasv), (rate_hbm, ratev), (convbc_hbm, conv_bc),
            (convx_hbm, conv_x), (skip_hbm, skipv), (gain_hbm, gainv),
        ))
    ]
    for copy in smalls[:5]:
        copy.start()
    load_b = pltpu.make_async_copy(b_hbm, bv, load_sem.at[pieces])
    load_c = pltpu.make_async_copy(c_hbm, cv, load_sem.at[pieces + 1])
    load_z = pltpu.make_async_copy(z_hbm, zv, load_sem.at[pieces + 2])
    load_b.start()
    for copy in smalls[5:]:
        copy.start()
    for p in range(pieces):
        pltpu.make_async_copy(x_hbm.at[:, pl.ds(p * LANES, LANES)], xv.at[p], load_sem.at[p]).start()
    load_c.start()
    load_z.start()
    def remote(src, dst, send, recv, device):
        return pltpu.make_async_remote_copy(
            src_ref=src, dst_ref=dst, send_sem=send, recv_sem=recv, device_id=device, device_id_type=MESH
        )

    tail_rows = pl.ds(tokens - MARGIN, MARGIN)
    margins = [
        remote(seg_hbm.at[:, pl.ds(tokens - LANES, LANES)], mseg, marg_send.at[0], marg_recv.at[0], ctx_of(1)),
        remote(b_hbm.at[tail_rows, :], mb, marg_send.at[1], marg_recv.at[1], ctx_of(1)),
        remote(x_hbm.at[tail_rows, :], mx, marg_send.at[2], marg_recv.at[2], ctx_of(1)),
        remote(c_hbm.at[tail_rows, :], mc, marg_send.at[3], marg_recv.at[3], ctx_of(1)),
    ]

    def margin(n):
        @pl.when(blk > 0)
        def _():
            margins[n].wait_recv()

    def state_copies(p, k):
        owner = {"ctx": 2 * p + k}
        return (
            remote(loc_out.at[p, k], loc_in.at[blk], l_send.at[p, k], l_recv.at[blk], owner),
            remote(t_out.at[p], t_in.at[blk], t_send.at[p, k], t_recv.at[blk], owner),
        )

    def state_waits(block):
        return (
            remote(loc_out.at[0, 0], loc_in.at[block], l_send.at[0, 0], l_recv.at[block], ctx_of(1)),
            remote(t_out.at[0], t_in.at[block], t_send.at[0, 0], t_recv.at[block], ctx_of(1)),
        )

    def carry_copy(block):
        return remote(
            c_out.at[block], c_in.at[blk // 2, lax.rem(blk, 2)], c_send.at[block], c_recv.at[blk // 2, lax.rem(blk, 2)],
            {"ctx": block},
        )

    def carry_wait(p, k):
        return remote(c_out.at[0], c_in.at[p, k], c_send.at[0], c_recv.at[p, k], ctx_of(1))

    def row_copy(p, d):
        return remote(
            sendbuf.at[p, pl.ds(d * share, share), :],
            recvbuf.at[me, p],
            o_send.at[d, p],
            o_recv.at[me, p],
            {"pipe": dest_sec, "head": d},
        )

    def row_wait(p, h):
        remote(
            sendbuf.at[p, pl.ds(0, share), :], recvbuf.at[h, p], o_send.at[0, p], o_recv.at[h, p],
            {"pipe": dest_sec, "head": 0},
        ).wait_recv()

    def scale_copy(d):
        return remote(scale_out.at[d], scale_in.at[me], s_send.at[d], s_recv.at[me], {"pipe": dest_sec, "head": d})

    def scale_wait(h):
        remote(
            scale_out.at[0], scale_in.at[h], s_send.at[0], s_recv.at[h], {"pipe": dest_sec, "head": 0}
        ).wait_recv()

    row_at = lax.broadcasted_iota(jnp.int32, (4 * heads, width), 0)
    lane_at = lax.broadcasted_iota(jnp.int32, (4 * heads, width), 1)
    mine = lax.rem(row_at, heads) == lane_at // (width // heads)
    inner_rows = mine & (row_at < 2 * heads)
    outer_rows = mine & (row_at >= 2 * heads)
    for p in range(pieces):
        lanes = slice(p * LANES, (p + 1) * LANES)
        spread_in[:, lanes] = inner_rows[:, lanes].astype(BF16)
        spread_out[:, lanes] = outer_rows[:, lanes].astype(BF16)

    @pl.when(blk == 0)
    def _():
        mx[...] = jnp.zeros_like(mx)
        mb[...] = jnp.zeros_like(mb)
        mc[...] = jnp.zeros_like(mc)
        mseg[...] = jnp.full_like(mseg, -1)

    for copy in smalls[:4]:
        copy.wait()
    eye = lax.broadcasted_iota(jnp.int32, (heads, heads), 0) == lax.broadcasted_iota(jnp.int32, (heads, heads), 1)
    bias = jnp.sum(jnp.where(eye, biasv[...], 0.0), axis=1, keepdims=True)
    rate = jnp.sum(jnp.where(eye, ratev[...], 0.0), axis=1, keepdims=True)
    raw = dtv[...] + bias
    steps = jnp.maximum(raw, 0.0) + jnp.log1p(jnp.exp(-jnp.abs(raw)))
    decay = -steps * rate
    high, rest = halves(decay)
    mid, low = halves(decay - high.astype(F32))
    split = jnp.concatenate([high, mid, low], axis=0)
    at = lax.broadcasted_iota(jnp.int32, (CHUNK, CHUNK), 0)
    of = lax.broadcasted_iota(jnp.int32, (CHUNK, CHUNK), 1)
    upper = (at <= of).astype(BF16)
    unit = (at == of).astype(BF16)
    for j in range(chunks):
        sums = nn(split[:, j * CHUNK : (j + 1) * CHUNK], upper)
        cum = sums[:heads] + sums[heads : 2 * heads] + sums[2 * heads :]
        in_high, in_low = halves(jnp.exp(-cum) * steps[:, j * CHUNK : (j + 1) * CHUNK])
        out_high, out_low = halves(jnp.exp(cum))
        both = jnp.concatenate([in_high, in_low, out_high, out_low], axis=0)
        fac[pl.ds(j * CHUNK, CHUNK), :] = nt(unit, both).astype(BF16)

    for n in range(tokens // LANES):
        segc[pl.ds(MARGIN + n * LANES, LANES), :] = column(segv[:, pl.ds(n * LANES, LANES)].astype(F32))

    pl.semaphore_wait(barrier, n_ctx - 1 + n_head)

    @pl.when(blk < n_ctx - 1)
    def _():
        for copy in margins:
            copy.start()

    def taps_of(r, size):
        here = segc[pl.ds(MARGIN + r, size), :]
        for j in range(1, 4):
            same = segc[pl.ds(MARGIN + r - j, size), :] == here
            taps[j - 1, pl.ds(r, size), :] = same.astype(F32)

    def conv_rows(w, r, size):
        total = w[3:4, :] * ext[pl.ds(MARGIN + r, size), :]
        for j in range(1, 4):
            shifted = ext[pl.ds(MARGIN + r - j, size), :]
            total = total + (w[3 - j : 4 - j, :] * shifted) * taps[j - 1, pl.ds(r, size), :]
        return silu(total)

    part = 64
    for copy in smalls[4:]:
        copy.wait()
    load_b.wait()
    ext[pl.ds(MARGIN, tokens), :] = bv[...].astype(F32)
    for r in range(part, tokens, part):
        taps_of(r, part)
        bv[pl.ds(r, part), :] = conv_rows(conv_bc[0], r, part).astype(BF16)
    margin(0)
    segc[pl.ds(0, MARGIN), :] = column(mseg[...].astype(F32))[LANES - MARGIN :, :]
    prior = segc[pl.ds(MARGIN - 1, 1), :]
    lasts = [segc[pl.ds(MARGIN + (j + 1) * CHUNK - 1, 1), :] for j in range(chunks)]
    taps_of(0, part)
    for r in range(0, tokens, LANES):
        taps[3, pl.ds(r, LANES), :] = (segc[pl.ds(MARGIN + r, LANES), :] == prior).astype(F32)
    margin(1)
    ext[pl.ds(0, MARGIN), :] = mb[...].astype(F32)
    bv[pl.ds(0, part), :] = conv_rows(conv_bc[0], 0, part).astype(BF16)
    for j in range(chunks):
        seg_t = segc[pl.ds(MARGIN + j * CHUNK, CHUNK), :]
        kept = jnp.where(seg_t == lasts[j], bv[pl.ds(j * CHUNK, CHUNK), :].astype(F32), 0.0)
        bmt[j] = kept.T.astype(BF16)

    def wide(row):
        return jnp.concatenate([row] * pieces, axis=1)

    rows = []
    for j in range(chunks):
        ends = nn(fac[pl.ds((j + 1) * CHUNK - 16, 16), :], spread_out[...])[15:16, :]
        rows.append(ends)
        if j > 0:
            rows.append(jnp.where(wide((lasts[j] == lasts[j - 1]).astype(F32)) > 0.5, ends, 0.0))
    total = rows[0] * rows[1] * rows[3]
    rows.append(jnp.where(wide((lasts[-1] == prior).astype(F32)) > 0.5, total, 0.0))
    skip_high, skip_low = halves(skipv[...])
    nothing = jnp.zeros((1, 2 * heads), BF16)
    skips = jnp.concatenate([nothing, skip_high, skip_low], axis=1)
    skips = jnp.concatenate([skips, jnp.zeros((15, 4 * heads), BF16)], axis=0)
    rows.append(nn(skips, spread_out[...])[0:1, :])
    rows.append(jnp.zeros((8 - len(rows), width), F32))
    rows_s[...] = jnp.concatenate(rows, axis=0)

    margin(2)

    def turned(step):
        away = (step + 1) // 2
        return lax.rem(blk // 2 + jnp.where(lax.rem(step, 2) == 1, away, pieces - away), pieces)

    @pl.loop(0, pieces)
    def _(turn):
        p = turned(pieces - 1 - turn)
        lanes = pl.ds(pl.multiple_of(p * LANES, LANES), LANES)
        pltpu.make_async_copy(x_hbm.at[:, lanes], xv.at[p], load_sem.at[p]).wait()
        ext[pl.ds(0, MARGIN), :] = mx[:, lanes].astype(F32)
        ext[pl.ds(MARGIN, tokens), :] = xv[p].astype(F32)
        w = conv_x[:, lanes]
        spread = spread_in[:, lanes]
        factors = rows_s[:, lanes]
        state, row = None, 0
        for j in range(chunks):
            for r in range(j * CHUNK, (j + 1) * CHUNK, part):
                span = pl.ds(r, part)
                value = conv_rows(w, r, part).astype(BF16)
                xs[p, span, :] = value
                xsc[p, span, :] = (value.astype(F32) * nn(fac[span, :], spread)).astype(BF16)
            own = nn(bmt[j], xsc[p, pl.ds(j * CHUNK, CHUNK), :])
            if j == 0:
                state = factors[row : row + 1, :] * own
                row += 1
            else:
                hid[p, j - 1] = state.astype(BF16)
                state = factors[row + 1 : row + 2, :] * state + factors[row : row + 1, :] * own
                row += 2
        through = factors[row : row + 1, :]

        for k in range(2):
            loc_out[p, k] = state[k * HALF : (k + 1) * HALF, :].astype(BF16)
        t_out[p] = through

        for k in range(2):
            owner = 2 * p + k

            @pl.when((blk < n_ctx - 1) & (owner != blk))
            def _():
                for copy in state_copies(p, k):
                    copy.start()

            @pl.when((blk < n_ctx - 1) & (owner == blk))
            def _():
                loc_in[blk] = state[k * HALF : (k + 1) * HALF, :].astype(BF16)
                t_in[blk] = through

    load_c.wait()
    margin(3)
    ext[pl.ds(0, MARGIN), :] = mc[...].astype(F32)
    ext[pl.ds(MARGIN, tokens), :] = cv[...].astype(F32)
    for r in range(0, tokens, part):
        cs[pl.ds(r, part), :] = conv_rows(conv_bc[1], r, part).astype(BF16)
    for j in range(chunks):
        span = pl.ds(j * CHUNK, CHUNK)
        seg_t = segc[pl.ds(MARGIN + j * CHUNK, CHUNK), :]
        for first in range(0, CHUNK, LANES):
            seg_u = segv[:, pl.ds(j * CHUNK + first, LANES)].astype(F32)
            score = nt(cs[span, :], bv[pl.ds(j * CHUNK + first, LANES), :])
            keep = (seg_t == seg_u) & (at[:, :LANES] >= of[:, :LANES] + first)
            smask[j, :, pl.ds(first, LANES)] = jnp.where(keep, score, 0.0).astype(BF16)
        if j > 0:
            kept = jnp.where(seg_t == lasts[j - 1], cs[span, :].astype(F32), 0.0)
            cmask[j - 1] = kept.astype(BF16)
    load_z.wait()

    ssq[...] = jnp.zeros_like(ssq)
    scale_out[...] = jnp.zeros_like(scale_out)

    @pl.loop(0, pieces)
    def _(p):
        lanes = pl.ds(pl.multiple_of(p * LANES, LANES), LANES)
        factors = rows_s[:, lanes]
        skip = factors[2 * chunks : 2 * chunks + 1, :]
        spread = spread_out[:, lanes]
        before = None
        for j in range(chunks):
            inner = nn(smask[j], xsc[p, pl.ds(j * CHUNK, CHUNK), :])
            if j > 0:
                inner = inner + nn(cmask[j - 1], hid[p, j - 1])
                end = factors[0:1, :] if j == 1 else factors[2 * j - 3 : 2 * j - 2, :]
                before = end if before is None else before * end
            for r in range(0, CHUNK, part):
                span = pl.ds(j * CHUNK + r, part)
                gate = silu(zv[span, lanes].astype(F32))
                grown = nn(fac[span, :], spread)
                mixed = grown * inner[r : r + part, :] + skip * xs[p, span, :].astype(F32)
                yg[p, span, :] = mixed * gate
                entry = grown * taps[3, span, :]
                if before is not None:
                    entry = entry * before
                eg[p, span, :] = entry * gate

    scan_s[...] = jnp.zeros_like(scan_s)

    @pl.loop(0, n_ctx - 1)
    def _(block):
        @pl.when(block != blk)
        def _():
            for copy in state_waits(block):
                copy.wait_recv()

        value = t_in[block] * scan_s[...] + loc_in[block].astype(F32)
        scan_s[...] = value
        c_out[block + 1] = value.astype(BF16)

        @pl.when(block + 1 != blk)
        def _():
            carry_copy(block + 1).start()

        @pl.when(block + 1 == blk)
        def _():
            c_in[blk // 2, lax.rem(blk, 2)] = value.astype(BF16)

    @pl.loop(0, pieces)
    def _(turn):
        p = turned(turn)
        lanes = pl.ds(pl.multiple_of(p * LANES, LANES), LANES)

        @pl.when(blk == 0)
        def _():
            car[...] = jnp.zeros_like(car)

        for k in range(2):

            @pl.when((blk > 0) & (2 * p + k != blk))
            def _():
                carry_wait(p, k).wait_recv()

            @pl.when(blk > 0)
            def _():
                car[pl.ds(k * HALF, HALF), :] = c_in[p, k]

        gain = gainv[:, lanes]
        state = car[...]
        for r in range(0, tokens, part):
            span = pl.ds(r, part)
            gated = yg[p, span, :] + eg[p, span, :] * nn(cs[span, :], state)
            ssq[span, :] += gated * gated
            sendbuf[p, span, :] = (gated * gain).astype(BF16)
        for other in range(n_head):
            row_copy(p, lax.rem(me + other, n_head)).start()

    for d in range(n_head):
        for n, first in enumerate((0, share - LANES)):
            total = jnp.sum(ssq[pl.ds(d * share + first, LANES), :].T, axis=0, keepdims=True)
            scale_out[d, pl.ds(n, 1), :] = lax.rsqrt(total * (1.0 / width) + 1e-05)
        scale_copy(d).start()

    @pl.loop(0, pieces)
    def _(p):
        for k in range(2):

            @pl.when((blk < n_ctx - 1) & (2 * p + k != blk))
            def _():
                for copy in state_copies(p, k):
                    copy.wait_send()

    @pl.loop(1, n_ctx)
    def _(block):
        @pl.when(block != blk)
        def _():
            carry_copy(block).wait_send()

    @pl.when(blk < n_ctx - 1)
    def _():
        for copy in margins:
            copy.wait_send()

    @pl.loop(0, pieces)
    def _(p):
        for h in range(n_head):
            row_copy(p, h).wait_send()
            row_wait(p, h)

    for h in range(n_head):
        scale_copy(h).wait_send()
        scale_wait(h)


def scaled(rows_hbm, scale_hbm, out_hbm, rows_v, scale_v, out_v, in_sem, out_sem):
    groups, pieces, share, _ = rows_v.shape
    width = pieces * LANES
    scales = pltpu.make_async_copy(scale_hbm, scale_v, in_sem.at[groups])
    scales.start()
    loads = [pltpu.make_async_copy(rows_hbm.at[g], rows_v.at[g], in_sem.at[g]) for g in range(groups)]
    stores = [
        pltpu.make_async_copy(
            out_v.at[:, pl.ds(g * width, width)], out_hbm.at[:, pl.ds(g * width, width)], out_sem.at[g]
        )
        for g in range(groups)
    ]
    for copy in loads:
        copy.start()
    scales.wait()
    rest = pl.ds(LANES, share - LANES)
    for g in range(groups):
        first = column(scale_v[g, pl.ds(0, 1), :])
        second = column(scale_v[g, pl.ds(1, 1), :])[2 * LANES - share :, :]
        loads[g].wait()
        for p in range(pieces):
            lanes = pl.ds(g * width + p * LANES, LANES)
            out_v[pl.ds(0, LANES), lanes] = (rows_v[g, p, pl.ds(0, LANES), :].astype(F32) * first).astype(BF16)
            out_v[rest, lanes] = (rows_v[g, p, rest, :].astype(F32) * second).astype(BF16)
        stores[g].start()
    for copy in stores:
        copy.wait()


def solution(mesh):
    sizes = tuple(mesh.shape[name] for name in ("pipe", "ctx", "head"))
    n_ctx, n_head = sizes[1:]

    def shards(
        x_in, b_in, c_in, z_in, dt_raw, seg_ids, conv_x, conv_bc, decay_rate, dt_bias, skip_d, norm_gain
    ):
        _, tokens, width = x_in.shape
        state = b_in.shape[2]
        heads = decay_rate.shape[1]
        pieces, chunks, share = width // LANES, tokens // CHUNK, tokens // n_head
        vmem, sem = pltpu.VMEM, pltpu.SemaphoreType.DMA
        scratch = [
            vmem((pieces, tokens, LANES), BF16),
            vmem((tokens, state), BF16),
            vmem((tokens, state), BF16),
            vmem((tokens, width), BF16),
            vmem((heads, tokens), F32),
            vmem((1, tokens), jnp.int32),
            vmem((4, width), F32),
            vmem((2, 4, state), F32),
            vmem((1, heads), F32),
            vmem((1, heads), F32),
            vmem((1, heads), F32),
            vmem((1, width), F32),
            vmem((MARGIN, width), BF16),
            vmem((MARGIN, state), BF16),
            vmem((MARGIN, state), BF16),
            vmem((1, LANES), jnp.int32),
            vmem((MARGIN + tokens, LANES), F32),
            vmem((MARGIN + tokens, LANES), F32),
            vmem((4, tokens, LANES), F32),
            vmem((tokens, 4 * heads), BF16),
            vmem((4 * heads, width), BF16),
            vmem((4 * heads, width), BF16),
            vmem((8, width), F32),
            vmem((chunks, state, CHUNK), BF16),
            vmem((chunks, CHUNK, CHUNK), BF16),
            vmem((tokens, state), BF16),
            vmem((chunks - 1, CHUNK, state), BF16),
            vmem((pieces, tokens, LANES), BF16),
            vmem((pieces, tokens, LANES), BF16),
            vmem((pieces, chunks - 1, state, LANES), BF16),
            vmem((pieces, tokens, LANES), F32),
            vmem((pieces, tokens, LANES), F32),
            vmem((tokens, LANES), F32),
            vmem((pieces, 2, HALF, LANES), BF16),
            vmem((pieces, 1, LANES), F32),
            vmem((n_ctx, HALF, LANES), BF16),
            vmem((n_ctx, 1, LANES), F32),
            vmem((HALF, LANES), F32),
            vmem((n_ctx, HALF, LANES), BF16),
            vmem((pieces, 2, HALF, LANES), BF16),
            vmem((state, LANES), BF16),
            vmem((pieces, tokens, LANES), BF16),
            vmem((n_head, 8, LANES), F32),
            sem((pieces + 3,)), sem((8,)),
            sem((4,)), sem((4,)),
            sem((pieces, 2)), sem((n_ctx,)),
            sem((pieces, 2)), sem((n_ctx,)),
            sem((n_ctx,)), sem((pieces, 2)),
            sem((n_head, pieces)), sem((n_head, pieces)),
            sem((n_head,)), sem((n_head,)),
        ]
        anywhere = pl.BlockSpec(memory_space=pl.ANY)
        rows, scales = pl.pallas_call(
            functools.partial(kernel, sizes),
            out_shape=(
                jax.ShapeDtypeStruct((n_head, pieces, share, LANES), BF16),
                jax.ShapeDtypeStruct((n_head, 8, LANES), F32),
            ),
            in_specs=[anywhere] * 12,
            out_specs=(anywhere, anywhere),
            scratch_shapes=scratch,
            compiler_params=pltpu.CompilerParams(collective_id=0, has_side_effects=True),
        )(
            x_in[0], b_in[0], c_in[0], z_in[0], dt_raw[0].T, seg_ids, conv_x[0], conv_bc[0],
            decay_rate, dt_bias, skip_d, norm_gain,
        )
        rows = pl.pallas_call(
            scaled,
            out_shape=jax.ShapeDtypeStruct((share, n_head * width), BF16),
            in_specs=[anywhere, anywhere],
            out_specs=anywhere,
            scratch_shapes=[
                vmem((n_head, pieces, share, LANES), BF16),
                vmem((n_head, 8, LANES), F32),
                vmem((share, n_head * width), BF16),
                sem((n_head + 1,)),
                sem((n_head,)),
            ],
        )(rows, scales)
        return rows[None]

    placed = (
        P("pipe", "ctx", "head"),
        P("pipe", "ctx", "head"),
        P("pipe", "ctx", "head"),
        P("pipe", "ctx", "head"),
        P("pipe", "ctx", "head"),
        P("pipe", "ctx"),
        P("pipe", None, "head"),
        P("pipe", None, None, "head"),
        P("pipe", "head"),
        P("pipe", "head"),
        P("pipe", "head"),
        P("pipe", "head"),
    )
    return jax.shard_map(
        shards,
        mesh=mesh,
        in_specs=placed,
        out_specs=P("pipe", ("ctx", "head"), None),
        check_vma=False,
    )
```

time: 65.5 us -> 60.7 us (0.927)
  the two profiles are of different devices: /device:TPU:361 before, /device:TPU:96 now
where the time goes in v2:
time: 60.7 us; the launch traced here: 60.5 us
  Pallas kernels  60.5 us (100%)
    pallas_call x1, Pallas kernels, shards(): pl.pallas_call(functools.partial(kernel, sizes), out_shape=(jax.ShapeDtyp...  58.2 us
    pallas_call x1, Pallas kernels, shards(): pl.pallas_call(scaled, out_shape=jax.ShapeDtypeStruct((share, n_head * wi...  2.36 us

profile of v2, /device:TPU:96, one launch (start us, length us, event | category | flops | bytes accessed | tf_op | source)
XLA Modules:
  0.0 60.5 jit_solution(14363005464446885694)
XLA Ops:
  0.0 58.2 %shard_map.118 = (bf16[4,8,192,128]{3,2,1,0:T(8,128)(2,1)}, f32[4,8,128]{2,1,0:T(8,128)}) custom-call(bf16[768,1024]{1,0:T(8,128)(2,1)} %bitcast.10, bf16[768,128]{1,0:T(8,128)(2,1)} %bitcast.12, bf16[768,128]{1,0:T(8,128)(2,1)} %bitcast.13, bf16[768,1024]{1,0:T(8,128)(2,1)} %bitcast.11, f32[16,768]{1,0:T(8,128)} %bitcast.14, s32[1,768]{1,0:T(1,128)} %seg_hbm.1, ...), custom_call_target="tpu_custom_call" | custom-call | tf_op jit(solution)/shard_map/pallas_call | solution.py:534
  58.2 2.4 %shard_map.119 = bf16[192,4096]{1,0:T(8,128)(2,1)} custom-call(bf16[4,8,192,128]{3,2,1,0:T(8,128)(2,1)} %get-tuple-element.7.rows_hbm, f32[4,8,128]{2,1,0:T(8,128)} %get-tuple-element.8.scale_hbm), custom_call_target="tpu_custom_call" | custom-call | tf_op jit(solution)/shard_map/pallas_call | solution.py:548

commit v3 on v2

--- a/solution.py
+++ b/solution.py
@@ -13,6 +13,7 @@
 CHUNK = 256
 LANES = 128
 MARGIN = 16
+EARLY = 5
 HALF = 64
 
 
@@ -363,13 +364,22 @@
         scan_s[...] = value
         c_out[block + 1] = value.astype(BF16)
 
-        @pl.when(block + 1 != blk)
+        @pl.when((block + 1 <= EARLY) & (block + 1 != blk))
         def _():
             carry_copy(block + 1).start()
 
-        @pl.when(block + 1 == blk)
+    @pl.when(blk > 0)
+    def _():
+        c_in[blk // 2, lax.rem(blk, 2)] = c_out[blk]
+
+    @pl.loop(1, n_ctx)
+    def _(step):
+        away = (step + 1) // 2
+        block = lax.rem(blk + jnp.where(lax.rem(step, 2) == 1, away, n_ctx - away), n_ctx)
+
+        @pl.when(block > EARLY)
         def _():
-            c_in[blk // 2, lax.rem(blk, 2)] = value.astype(BF16)
+            carry_copy(block).start()
 
     @pl.loop(0, pieces)
     def _(turn):

time: 60.7 us -> 60.3 us (level)
  the two profiles are of different devices: /device:TPU:96 before, /device:TPU:64 now
where the time goes in v3:
time: 60.3 us; the launch traced here: 60.1 us
  Pallas kernels  60.1 us (100%)
    pallas_call x1, Pallas kernels, shards(): pl.pallas_call(functools.partial(kernel, sizes), out_shape=(jax.ShapeDtyp...  57.8 us
    pallas_call x1, Pallas kernels, shards(): pl.pallas_call(scaled, out_shape=jax.ShapeDtypeStruct((share, n_head * wi...  2.36 us

profile of v3, /device:TPU:64, one launch (start us, length us, event | category | flops | bytes accessed | tf_op | source)
XLA Modules:
  0.0 60.1 jit_solution(12888453373186091043)
XLA Ops:
  0.0 57.8 %shard_map.118 = (bf16[4,8,192,128]{3,2,1,0:T(8,128)(2,1)}, f32[4,8,128]{2,1,0:T(8,128)}) custom-call(bf16[768,1024]{1,0:T(8,128)(2,1)} %bitcast.10, bf16[768,128]{1,0:T(8,128)(2,1)} %bitcast.12, bf16[768,128]{1,0:T(8,128)(2,1)} %bitcast.13, bf16[768,1024]{1,0:T(8,128)(2,1)} %bitcast.11, f32[16,768]{1,0:T(8,128)} %bitcast.14, s32[1,768]{1,0:T(1,128)} %seg_hbm.1, ...), custom_call_target="tpu_custom_call" | custom-call | tf_op jit(solution)/shard_map/pallas_call | solution.py:544
  57.8 2.4 %shard_map.119 = bf16[192,4096]{1,0:T(8,128)(2,1)} custom-call(bf16[4,8,192,128]{3,2,1,0:T(8,128)(2,1)} %get-tuple-element.7.rows_hbm, f32[4,8,128]{2,1,0:T(8,128)} %get-tuple-element.8.scale_hbm), custom_call_target="tpu_custom_call" | custom-call | tf_op jit(solution)/shard_map/pallas_call | solution.py:558
